TPU v7x, 32 devices: a whole 2x2x4 slice. The times are simulated.
32 devices in a mesh: ia: 4 (over x, core), ja: 8 (over z, y).
Axes of the slice: x: 2, y: 2, z: 4, core: 2. Of those that a mesh axis runs over, the one named last changes fastest.
Arguments:
- star_pos: float32 [3, 32768], P(None, ('ia', 'ja')), may hold values from -6 to 6
- star_vel: float32 [3, 32768], P(None, ('ia', 'ja')), may hold values from -3 to 3
- star_acc: float32 [3, 32768], P(None, ('ia', 'ja')), may hold values from -3 to 3
- star_jerk: float32 [3, 32768], P(None, ('ia', 'ja')), may hold values from -6 to 6
- star_mass: float32 [32768], P(('ia', 'ja')), may hold values from 6.1035157e-06 to 0.00015258789
- star_level: int32 [32768], P(('ia', 'ja')), may hold values from 0 to 5, as said below
- active_index: int32 [256], P(('ia', 'ja')), may hold values from 0 to 1023, as said below
- active_count: int32 [32], P(('ia', 'ja')), may hold values from 1 to 8, as said below
Outputs:
- updated: float32 [12, 256], P(None, ('ia', 'ja'))
Inputs may be any that keep to these rules, and one draw needn't show every extreme that they name: active_count[b] is the number of active stars of owner block b; some block has exactly 8, not always the same one. `active_index`: the slots of owner block b hold distinct local star numbers of that block; the first active_count[b] of them are exactly the stars of the block with star_level 3 or more, the others name inactive stars of the block. `star_level`: A star is active at this step exactly when its level is 3 or more.
All inputs are finite; a program needn't handle non-finite values.
Results may differ from a plain program's by a relative error of at most 0.0003.
Values sent between devices are 32-bit elements; how exact they have to be, the bound alone decides.
A program may use at most 64 MiB of HBM per device.

v0:
```python
import math
import jax
import jax.numpy as jnp
from jax import lax
from jax.sharding import PartitionSpec as P

tick_now = 44
top_level = 5
tick_length = 0.125
soft_square = 0.0001


def star_age(levels):
    periods = jnp.left_shift(jnp.ones_like(levels), top_level - levels)
    remains = jnp.remainder(jnp.full_like(levels, tick_now), periods)
    ticks = jnp.where(remains == 0, periods, remains)
    return ticks.astype(jnp.float32) * tick_length


def predict(positions, velocity, accelerations, jerk_rates, star_ages):
    elapsed = star_ages[None, :]
    new_pos = positions + elapsed * (
        velocity + elapsed * (accelerations * 0.5 + elapsed * jerk_rates / 6.0)
    )
    new_vel = velocity + elapsed * (accelerations + elapsed * jerk_rates * 0.5)
    return (new_pos, new_vel)


def pair_block(targets, sources):
    delta_pos = [sources[axis_num][None, :] - targets[axis_num][:, None] for axis_num in range(3)]
    delta_vel = [
        sources[3 + axis_num][None, :] - targets[3 + axis_num][:, None] for axis_num in range(3)
    ]
    squared = (
        delta_pos[0] * delta_pos[0]
        + delta_pos[1] * delta_pos[1]
        + delta_pos[2] * delta_pos[2]
        + soft_square
    )
    inverse = lax.rsqrt(squared)
    inverse_sq = inverse * inverse
    strength = sources[6][None, :] * inverse * inverse_sq
    radial = (
        3.0
        * (delta_pos[0] * delta_vel[0] + delta_pos[1] * delta_vel[1] + delta_pos[2] * delta_vel[2])
        * inverse_sq
    )
    results = [jnp.sum(strength * delta_pos[axis_num], axis=1) for axis_num in range(3)]
    results = results + [
        jnp.sum(strength * (delta_vel[axis_num] - radial * delta_pos[axis_num]), axis=1)
        for axis_num in range(3)
    ]
    return jnp.stack(results)


def correct(targets, forces, old_acc, old_jerk, step_sizes, live_mask):
    new_acc = forces[:3]
    new_jerk = forces[3:]
    elapsed = step_sizes[None, :]
    change = old_acc - new_acc
    snap_part = -6.0 * change - elapsed * (4.0 * old_jerk + 2.0 * new_jerk)
    crackle_part = 12.0 * change + 6.0 * elapsed * (old_jerk + new_jerk)
    cor_pos = targets[:3] + elapsed * elapsed * (snap_part / 24.0 + crackle_part / 120.0)
    cor_vel = targets[3:] + elapsed * (snap_part / 6.0 + crackle_part / 24.0)
    stacked = jnp.concatenate([cor_pos, cor_vel, new_acc, new_jerk], 0)
    return jnp.where(live_mask[None, :], stacked, 0.0)


def tile_forces(targets, sources):
    slot_count = targets.shape[1]
    source_count = sources.shape[1]
    tile_rows = math.gcd(slot_count, max(32, slot_count // 16))
    tile_cols = math.gcd(source_count, max(128, 131072 // tile_rows))
    tile_count = slot_count // tile_rows
    col_turns = source_count // tile_cols
    tiles = jnp.transpose(targets.reshape(6, tile_count, tile_rows), (1, 0, 2))
    offsets = jnp.arange(tile_count, dtype=jnp.int32) * tile_rows
    zero_tile = jnp.zeros((6, tile_rows), jnp.float32)

    def compute(target_tile):

        def advance(turn_index, running):
            source_part = lax.dynamic_slice_in_dim(sources, turn_index * tile_cols, tile_cols, 1)
            return running + pair_block(target_tile, source_part)

        return lax.fori_loop(0, col_turns, advance, zero_tile)

    def one_tile(tile_entry):
        target_tile, offset = tile_entry
        return compute(target_tile)

    results = lax.map(one_tile, (tiles, offsets))
    return jnp.transpose(results, (1, 0, 2)).reshape(6, slot_count)


def arrange(targets):
    return (targets, None, None)


def on_device(
    star_pos, star_vel, star_acc, star_jerk, star_mass, star_level, active_index, active_count
):
    capacity = active_index.shape[0]
    star_ages = star_age(star_level)
    pred_pos, pred_vel = predict(star_pos, star_vel, star_acc, star_jerk, star_ages)
    sources = jnp.concatenate([pred_pos, pred_vel, star_mass[None, :]], 0)
    own_targets = jnp.concatenate(
        [jnp.take(pred_pos, active_index, axis=1), jnp.take(pred_vel, active_index, axis=1)], 0
    )
    count_value = active_count.astype(jnp.float32)
    targets, counts = (
        lax.all_gather(own_targets, "ia", axis=1, tiled=True),
        lax.all_gather(count_value, "ia", axis=0, tiled=True),
    )
    prepared, live_total, places = arrange(targets)
    pair_sums = tile_forces(prepared, lax.all_gather(sources, "ja", axis=1, tiled=True))
    forces = lax.psum_scatter(pair_sums, "ia", scatter_dimension=1, tiled=True)
    live_mask = jnp.arange(capacity, dtype=jnp.int32) < active_count[0]
    old_acc = jnp.take(star_acc, active_index, axis=1)
    old_jerk = jnp.take(star_jerk, active_index, axis=1)
    step_sizes = jnp.take(star_ages, active_index)
    return correct(own_targets, forces, old_acc, old_jerk, step_sizes, live_mask)


def solution(mesh):
    placed = (
        P(None, ("ia", "ja")),
        P(None, ("ia", "ja")),
        P(None, ("ia", "ja")),
        P(None, ("ia", "ja")),
        P(("ia", "ja")),
        P(("ia", "ja")),
        P(("ia", "ja")),
        P(("ia", "ja")),
    )
    return jax.shard_map(
        on_device, mesh=mesh, in_specs=placed, out_specs=P(None, ("ia", "ja")), check_vma=False
    )
```

profile of v0, /device:TPU:0, one launch (start us, length us, event | category | flops | bytes accessed | tf_op | source)
XLA Modules:
  0.0 60.1 jit_solution(17922956348764657168)
XLA Ops:
  0.0 0.0 copy-start.5
  0.0 0.7 %compare_select_fusion.2 = s32[8]{0:T(128)S(1)} fusion(s32[8]{0:T(128)} %param.18), kind=kLoop, calls=%fused_computation.75 | loop fusion | flops 24 | bytes 64 | tf_op jit(solution)/shard_map/jit(_take)/jit(_where)/select_n | solution.py:108
  0.7 0.0 copy-done.5
  0.7 0.1 fusion.18
  0.8 0.0 copy-start.6
  0.8 0.0 copy-start
  0.8 0.0 copy-start.1
  0.9 0.0 copy-start.2
  0.9 0.0 copy-start.3
  0.9 0.6 %gather_fusion = f32[8]{0:T(128)S(1)} fusion(f32[1024]{0:T(1024)S(1)} %fusion.18, s32[1024]{0:T(1024)S(1)} %pad_clamp_fusion), kind=kCustom, calls=%fused_computation.4 | custom fusion | bytes 96 | tf_op jit(solution)/shard_map/jit(_take)/gather | solution.py:121
  1.5 0.0 copy-done.6
  1.5 0.0 copy-done
  1.6 0.0 copy-done.1
  1.6 0.0 copy-done.2
  1.6 0.0 copy-done.3
  1.6 0.2 copy.76
  1.9 0.6 gather_fusion.1
  2.4 0.2 copy.78
  2.6 0.6 gather_fusion.3
  3.2 0.1 select_bitcast_fusion.1
  3.3 0.1 pad_maximum_fusion.1
  3.4 6.2 %all_gather.7 = f32[6,32]{0,1:T(8,128)S(1)} all-gather(f32[6,8]{0,1:T(8,128)S(1)} %pad_maximum_fusion.1), channel_id=1, replica_groups=mesh['ia'=4,'ja'=8] {'ia'}, dimensions={1}, use_global_device_ids=true | all-gather | bytes 960 | tf_op jit(solution)/shard_map/all_gather | solution.py:112
  9.6 0.0 copy-start.4
  9.6 0.1 copy.79
  9.7 0.6 %copy-done.4 = f32[1024]{0:T(1024)S(1)} copy-done((f32[1024]{0:T(1024)S(1)}, f32[1024]{0:T(1024)}, u32[]{:S(2)}) %copy-start.4) | copy-done | bytes 4120
  10.3 31.6 %all_gather.6 = f32[7,8192]{1,0:T(8,128)S(1)} all-gather(f32[7,1024]{1,0:T(8,128)S(1)} %pad_maximum_fusion), channel_id=1, replica_groups=mesh['ia'=4,'ja'=8] {'ja'}, dimensions={1}, use_global_device_ids=true | all-gather | bytes 258048 | tf_op jit(solution)/shard_map/all_gather | solution.py:116
  41.9 3.0 %while.21 = (s32[]{:T(128)}, f32[6,32]{1,0:T(8,128)S(1)}, f32[7,8192]{1,0:T(8,128)S(1)}, f32[6,32]{1,0:T(8,128)S(1)}, s32[]{:T(128)}, /*index=5*/s32[]{:T(128)},...) while((s32[]{:T(128)}, f32[6,32]{1,0:T(8,128)S(1)}, ...), condition=%wide.region_7.9_spmd.clone, body=%wide.region_0.8_spmd.clone.sunk | while | flops 5243085 | bytes 351265 | solution.py:86
  41.9 0.3 fusion.33
  42.2 1.1 %fusion.34 = (f32[32]{0:T(128)S(1)}, f32[32]{0:T(128)S(1)}, f32[32]{0:T(128)S(1)}, f32[32]{0:T(128)S(1)}, f32[32]{0:T(128)S(1)}, /*index=5*/f32[32]{0:T(128)S(1)}) fusion(f32[32]{0:T(128)S(1)} %get-tuple-element.220, f32[4096]{0:T(1024)S(1)} %bitcast.90, f32[32]{0:T(128)S(1)} %get-tuple-element.222, f32[4096]{0:T(1024)S(1)} %bitcast.86, ...), kind=kLoop, calls=%fused_computation.25.clone.1 | loop fusion | flops 5242688 | bytes 116224 | tf_op jit(solution)/shard_map/while/body/eval_jaxpr/while/body/eval_jaxpr/reduce_sum | solution.py:50
  43.4 0.3 fusion.33
  43.7 1.1 %fusion.34 = (f32[32]{0:T(128)S(1)}, f32[32]{0:T(128)S(1)}, f32[32]{0:T(128)S(1)}, f32[32]{0:T(128)S(1)}, f32[32]{0:T(128)S(1)}, /*index=5*/f32[32]{0:T(128)S(1)}) fusion(f32[32]{0:T(128)S(1)} %get-tuple-element.220, f32[4096]{0:T(1024)S(1)} %bitcast.90, f32[32]{0:T(128)S(1)} %get-tuple-element.222, f32[4096]{0:T(1024)S(1)} %bitcast.86, ...), kind=kLoop, calls=%fused_computation.25.clone.1 | loop fusion | flops 5242688 | bytes 116224 | tf_op jit(solution)/shard_map/while/body/eval_jaxpr/while/body/eval_jaxpr/reduce_sum | solution.py:50
  44.9 0.1 copy.80
  45.0 10.1 %all-reduce = f32[6,32]{0,1:T(8,128)S(1)} all-reduce(f32[6,32]{0,1:T(8,128)S(1)} %copy.80), channel_id=2, replica_groups=mesh['ia'=4,'ja'=8] {'ia'}, use_global_device_ids=true, to_apply=%region_8.10.clone | all-reduce | flops 192 | bytes 1536
  55.1 0.0 copy-start.7
  55.1 0.7 %copy-done.7 = u32[32]{0:T(128)S(1)} copy-done((u32[32]{0:T(128)S(1)}, u32[32]{0:T(128)}, u32[]{:S(2)}) %copy-start.7) | copy-done | bytes 152
  55.8 0.6 dynamic-slice.1
  57.0 0.2 copy.77
  57.3 0.6 gather_fusion.2
  57.8 0.2 copy.81
  58.1 0.6 gather_fusion.4
  58.6 0.1 multiply_add_fusion.3
  58.7 0.1 multiply_add_fusion.2
  59.4 0.7 %maximum_select_fusion = f32[12,8]{0,1:T(8,128)} fusion(f32[6,8]{0,1:T(8,128)S(1)} %constant_dynamic-slice_fusion.1, f32[3,8]{0,1:T(8,128)S(1)} %multiply_add_fusion.2, f32[3,8]{0,1:T(8,128)S(1)} %get-tuple-element.153, pred[8]{0:T(512)(128)(4,1)S(1)} %iota_compare_fusion), kind=kLoop, calls=%fused_computation.58 | loop fusion | flops 288 | bytes 776 | tf_op jit(solution)/shard_map/jit(_where)/select_n | solution.py:66
  (14 shorter events, 0.1 us)
Async XLA Ops:
  0.0 0.7 %copy-start.5 = (s32[1024]{0:T(1024)S(1)}, s32[1024]{0:T(1024)}, u32[]{:S(2)}) copy-start(s32[1024]{0:T(1024)} %param.17) | copy-start | bytes 12292
  0.8 0.7 %copy-start.6 = (s32[8]{0:T(128)S(1)}, s32[8]{0:T(128)}, u32[]{:S(2)}) copy-start(s32[8]{0:T(128)} %param.18) | copy-start | bytes 100
  0.8 0.7 %copy-start = (f32[3,1024]{1,0:T(4,128)S(1)}, f32[3,1024]{1,0:T(4,128)}, u32[]{:S(2)}) copy-start(f32[3,1024]{1,0:T(4,128)} %param.14) | copy-start | bytes 36868
  0.8 0.7 %copy-start.1 = (f32[3,1024]{1,0:T(4,128)S(1)}, f32[3,1024]{1,0:T(4,128)}, u32[]{:S(2)}) copy-start(f32[3,1024]{1,0:T(4,128)} %param.15) | copy-start | bytes 36868
  0.9 0.7 %copy-start.2 = (f32[3,1024]{1,0:T(4,128)S(1)}, f32[3,1024]{1,0:T(4,128)}, u32[]{:S(2)}) copy-start(f32[3,1024]{1,0:T(4,128)} %param.12) | copy-start | bytes 36868
  0.9 0.7 %copy-start.3 = (f32[3,1024]{1,0:T(4,128)S(1)}, f32[3,1024]{1,0:T(4,128)}, u32[]{:S(2)}) copy-start(f32[3,1024]{1,0:T(4,128)} %param.13) | copy-start | bytes 36868
  9.6 0.7 %copy-start.4 = (f32[1024]{0:T(1024)S(1)}, f32[1024]{0:T(1024)}, u32[]{:S(2)}) copy-start(f32[1024]{0:T(1024)} %param.16) | copy-start | bytes 12292
  55.1 0.7 %copy-start.7 = (u32[32]{0:T(128)S(1)}, u32[32]{0:T(128)}, u32[]{:S(2)}) copy-start(u32[32]{0:T(128)} %constant.128) | copy-start | bytes 388
where the time goes:
time: 60.5 us; the launch traced here: 60.1 us
  blocking collectives  48 us (79%)
  local copies, waits for them, and re-layouts  6.49 us (11%)
  other arithmetic  4.14 us (7%)
  between operations  1.45 us (2%)
    all_gather x1, blocking collectives, on_device(): lax.all_gather(sources, 'ja', axis=1, tiled=True)  31.6 us
    unnamed x1, blocking collectives  10.1 us
    all_gather x1, blocking collectives, on_device(): lax.all_gather(own_targets, 'ia', axis=1, tiled=True)  6.23 us
    unnamed x21, local copies, waits for them, and re-layouts  2.47 us
    reduce_sum x2, other arithmetic, pair_block(): jnp.sum(strength * (delta_vel[axis_num] - radial * delta_pos[axis_num]),...  2.3 us

commit v1 on v0

--- a/solution.py
+++ b/solution.py
@@ -8,6 +8,18 @@
 top_level = 5
 tick_length = 0.125
 soft_square = 0.0001
+
+
+def doubled_up(value, axis, dim):
+    ways, here = (lax.axis_size(axis), lax.axis_index(axis))
+    grown, reach = (value, 1)
+    while reach < ways:
+        theirs = lax.ppermute(grown, axis, [(d, d ^ reach) for d in range(ways)])
+        mine_first = jnp.concatenate([grown, theirs], axis=dim)
+        theirs_first = jnp.concatenate([theirs, grown], axis=dim)
+        grown = jnp.where(here & reach == 0, mine_first, theirs_first)
+        reach = 2 * reach
+    return grown
 
 
 def star_age(levels):
@@ -109,7 +121,7 @@
     )
     count_value = active_count.astype(jnp.float32)
     targets, counts = (
-        lax.all_gather(own_targets, "ia", axis=1, tiled=True),
+        doubled_up(own_targets, "ia", 1),
         lax.all_gather(count_value, "ia", axis=0, tiled=True),
     )
     prepared, live_total, places = arrange(targets)

time: 60.5 us -> 57.3 us (0.947)
  blocking collectives: 48 us -> 42.3 us
  starting transfers between devices: 0 us -> 2 us
  waiting for transfers between devices: 0 us -> 0.72 us
    all_gather x1 -> x0, blocking collectives: 6.23 us -> none  [on_device(): lax.all_gather(own_targets, 'ia', axis=1, tiled=True)]
    ppermute x0 -> x2, starting transfers between devices: none -> 2 us  [doubled_up(): theirs = lax.ppermute(grown, axis, [(d, d ^ reach) for d in range(ways)])]
    ppermute x0 -> x2, waiting for transfers between devices: none -> 0.72 us  [doubled_up(): theirs = lax.ppermute(grown, axis, [(d, d ^ reach) for d in range(ways)])]
    unnamed x21 -> x20, local copies, waits for them, and re-layouts: 2.47 us -> 1.89 us
  transfers between devices with their start and end apart: 0 -> 2, of which waited for: 0 -> 1; matrix products, arithmetic and copies ran while one was open for 0% -> 4% of each run, Pallas kernels for 0% -> 0%
where the time goes in v1:
time: 57.3 us; the launch traced here: 56.9 us
  blocking collectives  42.3 us (74%)
  local copies, waits for them, and re-layouts  6.06 us (11%)
  other arithmetic  4.31 us (8%)
  starting transfers between devices  2 us (3%)
  between operations  1.5 us (3%)
  waiting for transfers between devices  0.72 us (1%)
    all_gather x1, blocking collectives, on_device(): lax.all_gather(sources, 'ja', axis=1, tiled=True)  32.2 us
    unnamed x1, blocking collectives  10.1 us
    reduce_sum x2, other arithmetic, pair_block(): jnp.sum(strength * (delta_vel[axis_num] - radial * delta_pos[axis_num]),...  2.3 us
    ppermute x2, starting transfers between devices, doubled_up(): theirs = lax.ppermute(grown, axis, [(d, d ^ reach) for d in range(ways)])  2 us
    unnamed x20, local copies, waits for them, and re-layouts  1.89 us
  transfers between devices with their start and end apart: 2, of which 1 were waited for; matrix products, arithmetic and copies ran while one was open for 4% of the time, Pallas kernels for 0%

profile of v1, /device:TPU:0, one launch (start us, length us, event | category | flops | bytes accessed | tf_op | source)
XLA Modules:
  0.0 56.9 jit_solution(12635065567360904768)
XLA Ops:
  0.0 0.0 copy-start.5
  0.0 0.7 %compare_select_fusion.2 = s32[8]{0:T(128)S(1)} fusion(s32[8]{0:T(128)} %param.18), kind=kLoop, calls=%fused_computation.77 | loop fusion | flops 24 | bytes 64 | tf_op jit(solution)/shard_map/jit(_take)/jit(_where)/select_n | solution.py:120
  0.7 0.0 copy-done.5
  0.7 0.1 fusion.18
  0.8 0.0 copy-start.6
  0.8 0.0 copy-start
  0.8 0.0 copy-start.1
  0.9 0.0 copy-start.2
  0.9 0.0 copy-start.3
  0.9 0.6 %gather_fusion = f32[8]{0:T(128)S(1)} fusion(f32[1024]{0:T(1024)S(1)} %fusion.18, s32[1024]{0:T(1024)S(1)} %pad_clamp_fusion), kind=kCustom, calls=%fused_computation.4 | custom fusion | bytes 96 | tf_op jit(solution)/shard_map/jit(_take)/gather | solution.py:133
  1.5 0.0 copy-done.6
  1.5 0.0 copy-done
  1.6 0.0 copy-done.1
  1.6 0.0 copy-done.2
  1.6 0.0 copy-done.3
  1.6 0.2 copy.82
  1.9 0.6 gather_fusion.1
  2.4 0.2 copy.84
  2.6 0.6 gather_fusion.3
  3.2 0.1 select_bitcast_fusion.1
  3.3 0.1 pad_maximum_fusion.1
  3.4 0.5 collective-permute-start
  3.9 0.2 copy.83
  4.1 0.2 copy.90
  4.3 0.0 copy-start.4
  4.3 0.7 %copy-done.4 = f32[1024]{0:T(1024)S(1)} copy-done((f32[1024]{0:T(1024)S(1)}, f32[1024]{0:T(1024)}, u32[]{:S(2)}) %copy-start.4) | copy-done | bytes 4120
  5.0 32.2 %all_gather.3 = f32[7,8192]{1,0:T(8,128)S(1)} all-gather(f32[7,1024]{1,0:T(8,128)S(1)} %pad_maximum_fusion), channel_id=1, replica_groups=mesh['ia'=4,'ja'=8] {'ja'}, dimensions={1}, use_global_device_ids=true | all-gather | bytes 258048 | tf_op jit(solution)/shard_map/all_gather | solution.py:128
  37.2 0.6 gather_fusion.2
  38.4 0.6 gather_fusion.4
  39.0 0.0 collective-permute-done
  39.0 0.1 maximum_select_fusion
  39.1 1.5 %collective-permute-start.1 = (f32[6,16]{0,1:T(8,128)S(1)}, f32[6,16]{0,1:T(8,128)S(1)}, u32[]{:S(2)}, u32[]{:S(2)}) collective-permute-start(f32[6,16]{0,1:T(8,128)S(1)} %maximum_select_fusion), channel_id=1, source_target_pairs={{0,16},{8,24},{16,0},{24,8},{1,17},{9,25},{17,1},{25,9},{2,18},{10... | collective-permute-start | bytes 1160 | tf_op jit(solution)/shard_map/ppermute | solution.py:17
  40.6 0.0 copy-done.7
  40.6 0.7 %dynamic-slice.1 = u32[1]{0:T(128)} dynamic-slice(u32[32]{0:T(128)S(1)} %copy-done.7, u32[]{:T(128)S(6)} %add.147), dynamic_slice_sizes={1} | dynamic-slice | bytes 12
  41.9 0.1 copy.85
  42.0 0.7 %collective-permute-done.1 = f32[6,16]{0,1:T(8,128)S(1)} collective-permute-done((f32[6,16]{0,1:T(8,128)S(1)}, f32[6,16]{0,1:T(8,128)S(1)}, u32[]{:S(2)}, u32[]{:S(2)}) %collective-permute-start.1) | collective-permute-done | bytes 416 | tf_op jit(solution)/shard_map/ppermute | solution.py:17
  42.7 0.1 copy.86
  42.8 0.1 maximum_select_fusion.1
  42.9 3.0 %while.21 = (s32[]{:T(128)}, f32[6,32]{1,0:T(8,128)S(1)}, f32[7,8192]{1,0:T(8,128)S(1)}, f32[6,32]{1,0:T(8,128)S(1)}, s32[]{:T(128)}, /*index=5*/s32[]{:T(128)},...) while((s32[]{:T(128)}, f32[6,32]{1,0:T(8,128)S(1)}, ...), condition=%wide.region_7.9_spmd.clone, body=%wide.region_0.8_spmd.clone.sunk | while | flops 5243085 | bytes 351265 | solution.py:98
  42.9 0.3 fusion.33
  43.2 1.1 %fusion.34 = (f32[32]{0:T(128)S(1)}, f32[32]{0:T(128)S(1)}, f32[32]{0:T(128)S(1)}, f32[32]{0:T(128)S(1)}, f32[32]{0:T(128)S(1)}, /*index=5*/f32[32]{0:T(128)S(1)}) fusion(f32[32]{0:T(128)S(1)} %get-tuple-element.208, f32[4096]{0:T(1024)S(1)} %bitcast.90, f32[32]{0:T(128)S(1)} %get-tuple-element.210, f32[4096]{0:T(1024)S(1)} %bitcast.86, ...), kind=kLoop, calls=%fused_computation.25.clone.1 | loop fusion | flops 5242688 | bytes 116224 | tf_op jit(solution)/shard_map/while/body/eval_jaxpr/while/body/eval_jaxpr/reduce_sum | solution.py:62
  44.4 0.3 fusion.33
  44.7 1.1 %fusion.34 = (f32[32]{0:T(128)S(1)}, f32[32]{0:T(128)S(1)}, f32[32]{0:T(128)S(1)}, f32[32]{0:T(128)S(1)}, f32[32]{0:T(128)S(1)}, /*index=5*/f32[32]{0:T(128)S(1)}) fusion(f32[32]{0:T(128)S(1)} %get-tuple-element.208, f32[4096]{0:T(1024)S(1)} %bitcast.90, f32[32]{0:T(128)S(1)} %get-tuple-element.210, f32[4096]{0:T(1024)S(1)} %bitcast.86, ...), kind=kLoop, calls=%fused_computation.25.clone.1 | loop fusion | flops 5242688 | bytes 116224 | tf_op jit(solution)/shard_map/while/body/eval_jaxpr/while/body/eval_jaxpr/reduce_sum | solution.py:62
  45.9 0.1 copy.89
  46.0 10.1 %all-reduce = f32[6,32]{0,1:T(8,128)S(1)} all-reduce(f32[6,32]{0,1:T(8,128)S(1)} %copy.89), channel_id=2, replica_groups=mesh['ia'=4,'ja'=8] {'ia'}, use_global_device_ids=true, to_apply=%region_8.10.clone | all-reduce | flops 192 | bytes 1536
  56.1 0.1 multiply_add_fusion.3
  56.2 0.1 multiply_add_fusion.2
  56.2 0.7 %maximum_select_fusion.2 = f32[12,8]{0,1:T(8,128)} fusion(f32[6,8]{0,1:T(8,128)S(1)} %constant_dynamic-slice_fusion.1, f32[3,8]{0,1:T(8,128)S(1)} %multiply_add_fusion.2, f32[3,8]{0,1:T(8,128)S(1)} %get-tuple-element.141, pred[8]{0:T(512)(128)(4,1)S(1)} %iota_compare_fusion), kind=kLoop, calls=%fused_computation.60 | loop fusion | flops 288 | bytes 776 | tf_op jit(solution)/shard_map/jit(_where)/select_n | solution.py:78
  (15 shorter events, 0.1 us)
Async XLA Ops:
  0.0 0.7 %copy-start.5 = (s32[1024]{0:T(1024)S(1)}, s32[1024]{0:T(1024)}, u32[]{:S(2)}) copy-start(s32[1024]{0:T(1024)} %param.17) | copy-start | bytes 12292
  0.8 0.7 %copy-start.6 = (s32[8]{0:T(128)S(1)}, s32[8]{0:T(128)}, u32[]{:S(2)}) copy-start(s32[8]{0:T(128)} %param.18) | copy-start | bytes 100
  0.8 0.7 %copy-start = (f32[3,1024]{1,0:T(4,128)S(1)}, f32[3,1024]{1,0:T(4,128)}, u32[]{:S(2)}) copy-start(f32[3,1024]{1,0:T(4,128)} %param.14) | copy-start | bytes 36868
  0.8 0.7 %copy-start.1 = (f32[3,1024]{1,0:T(4,128)S(1)}, f32[3,1024]{1,0:T(4,128)}, u32[]{:S(2)}) copy-start(f32[3,1024]{1,0:T(4,128)} %param.15) | copy-start | bytes 36868
  0.9 0.7 %copy-start.2 = (f32[3,1024]{1,0:T(4,128)S(1)}, f32[3,1024]{1,0:T(4,128)}, u32[]{:S(2)}) copy-start(f32[3,1024]{1,0:T(4,128)} %param.12) | copy-start | bytes 36868
  0.9 0.7 %copy-start.3 = (f32[3,1024]{1,0:T(4,128)S(1)}, f32[3,1024]{1,0:T(4,128)}, u32[]{:S(2)}) copy-start(f32[3,1024]{1,0:T(4,128)} %param.13) | copy-start | bytes 36868
  3.4 35.6 %collective-permute-start = (f32[6,8]{0,1:T(8,128)S(1)}, f32[6,8]{0,1:T(8,128)S(1)}, u32[]{:S(2)}, u32[]{:S(2)}) collective-permute-start(f32[6,8]{0,1:T(8,128)S(1)} %pad_maximum_fusion.1), channel_id=1, source_target_pairs={{0,8},{8,0},{16,24},{24,16},{1,9},{9,1},{17,25},{25,17},{2,10},{10... | collective-permute-start | bytes 584 | tf_op jit(solution)/shard_map/ppermute | solution.py:17
  4.3 0.7 %copy-start.4 = (f32[1024]{0:T(1024)S(1)}, f32[1024]{0:T(1024)}, u32[]{:S(2)}) copy-start(f32[1024]{0:T(1024)} %param.16) | copy-start | bytes 12292
  39.1 1.5 %copy-start.7 = (u32[32]{0:T(128)S(1)}, u32[32]{0:T(128)}, u32[]{:S(2)}) copy-start(u32[32]{0:T(128)} %constant.136) | copy-start | bytes 388
  39.1 3.7 %collective-permute-start.1 = (f32[6,16]{0,1:T(8,128)S(1)}, f32[6,16]{0,1:T(8,128)S(1)}, u32[]{:S(2)}, u32[]{:S(2)}) collective-permute-start(f32[6,16]{0,1:T(8,128)S(1)} %maximum_select_fusion), channel_id=1, source_target_pairs={{0,16},{8,24},{16,0},{24,8},{1,17},{9,25},{17,1},{25,9},{2,18},{10... | collective-permute-start | bytes 1160 | tf_op jit(solution)/shard_map/ppermute | solution.py:17
